TPU v7x, 32 devices: a whole 2x2x4 slice. The times are simulated.
32 devices in a mesh: groups: 2 (over x), head: 16 (over z, y, core).
Axes of the slice: x: 2, y: 2, z: 4, core: 2. Of those that a mesh axis runs over, the one named last changes fastest.
Arguments:
- queries: bfloat16 [256, 2048], P('groups', 'head'), parts along dimension 0, may hold values from -400 to 400
- cache: bfloat16 [2, 8192, 128], P(None, ('groups', 'head')), parts along dimension 1, may hold values from -5 to 5
- cache_scale: bfloat16 [2, 1, 8192], P(None, None, ('groups', 'head')), parts along dimension 2, may hold values from 0.5 to 4
- offsets: int32 [4], P('groups'), parts along dimension 0, may hold values from 0 to 2048, as said below
- lengths: int32 [4], P('groups'), parts along dimension 0, may hold values from 64 to 2048, as said below
- clamp_code: int32 [2], P('groups'), parts along dimension 0, may hold values from 512 to 1535
- w_out: bfloat16 [2048, 16384], P('head'), may hold values from -0.125 to 0.125
Outputs:
- projected: bfloat16 [16384, 256], P('head', 'groups'), parts along dimension 1
There are 2 independent parts, one for each index of `groups`. A program takes and returns all parts, laid end to end along the dimension named above; an argument that names none is the same for every part. Nothing has to cross between parts.
Inputs may be any that keep to these rules, and one draw needn't show every extreme that they name: Request r's cache region is offsets[r] to offsets[r] + lengths[r] - 1 and lies within positions r * 2048 to (r + 1) * 2048 - 1. `lengths`: the last 64 positions of each region hold the span's own keys and values; in every draw some request's length is exactly 2048.
All inputs are finite; a program needn't handle non-finite values.
Results may differ from a plain program's by a relative error of at most 0.0068.
Values may be sent and summed in bfloat16 or wider, within the bound.
No kernel may reach another device: no remote copies, remote signals or barrier semaphores. Data moves between devices by JAX's collectives and lax.ppermute only.
A program may use at most 128 MiB of HBM per device.

v0:
```python
import math
import jax
import jax.numpy as jnp
from jax import lax
from jax.sharding import PartitionSpec as P

SPAN = 64
NEG_FILL = -1e30


def hadamard(matrix_size):
    counter_index = jnp.arange(matrix_size, dtype=jnp.int32)
    common = counter_index[:, None] & counter_index[None, :]
    parity = jnp.zeros((matrix_size, matrix_size), jnp.int32)
    for bit_place in range(matrix_size.bit_length() - 1):
        parity = parity + (common >> bit_place & 1)
    return jnp.where(parity % 2 == 0, 1.0, -1.0).astype(jnp.float32)


def masked_scores(query_block, key_rows, key_scale, visible_tile, inv_root):
    scores = jnp.einsum("tjd,pd->jtp", query_block, key_rows, preferred_element_type=jnp.float32)
    scores = scores * (key_scale.astype(jnp.float32) * inv_root)[None, None, :]
    return jnp.where(visible_tile[None], scores, NEG_FILL)


def tile_sums(masked, row_max, visible_tile, value_scale, value_rows):
    weights = jnp.where(visible_tile[None], jnp.exp(masked - row_max[..., None]), 0.0)
    prob_rows = (weights * value_scale.astype(jnp.float32)[None, None, :]).astype(jnp.bfloat16)
    numerator = jnp.einsum("jtp,pd->jtd", prob_rows, value_rows, preferred_element_type=jnp.float32)
    return (numerator, jnp.sum(weights, axis=2))


def per_device(queries, cache, cache_scale, offsets, lengths, clamp_code, w_out):
    my_index = lax.axis_index("head")
    head_dim = queries.shape[1]
    local_len = cache.shape[1]
    kv_count = cache.shape[2] // head_dim
    gathered = lax.all_gather(queries, "head", axis=1, tiled=True)
    tok_rows = gathered.shape[0]
    head_count = gathered.shape[1] // head_dim
    per_group = head_count // kv_count
    token_ids = jnp.arange(tok_rows, dtype=jnp.int32)
    request = token_ids // SPAN
    within = token_ids % SPAN
    req_match = request[:, None] == jnp.arange(offsets.shape[0], dtype=jnp.int32)[None, :]
    starts = jnp.sum(jnp.where(req_match, offsets[None, :], 0), axis=1)
    last_pos = starts + jnp.sum(jnp.where(req_match, lengths[None, :], 0), axis=1) - SPAN + within
    inv_root = 1.0 / math.sqrt(head_dim)
    positions = my_index * local_len + jnp.arange(local_len, dtype=jnp.int32)
    visible = (positions[None, :] >= starts[:, None]) & (positions[None, :] <= last_pos[:, None])
    max_parts = []
    for kv_index in range(kv_count):
        column_left = kv_index * head_dim
        query_block = gathered[
            :, column_left * per_group : (column_left + head_dim) * per_group
        ].reshape(tok_rows, per_group, head_dim)
        masked = masked_scores(
            query_block,
            cache[0, :, column_left : column_left + head_dim],
            cache_scale[0, kv_index],
            visible,
            inv_root,
        )
        max_parts.append(jnp.max(masked, axis=2))
    local_max = jnp.concatenate(max_parts, 0)
    global_max = lax.pmax(local_max, "head")
    numer_parts = []
    denom_parts = []
    for kv_index in range(kv_count):
        column_left = kv_index * head_dim
        query_block = gathered[
            :, column_left * per_group : (column_left + head_dim) * per_group
        ].reshape(tok_rows, per_group, head_dim)
        masked = masked_scores(
            query_block,
            cache[0, :, column_left : column_left + head_dim],
            cache_scale[0, kv_index],
            visible,
            inv_root,
        )
        row_max = global_max[kv_index * per_group : (kv_index + 1) * per_group]
        numer_part, denom_part = tile_sums(
            masked,
            row_max,
            visible,
            cache_scale[1, kv_index],
            cache[1, :, column_left : column_left + head_dim],
        )
        numer_parts.append(numer_part)
        denom_parts.append(denom_part)
    numerator = jnp.concatenate(numer_parts, 0)
    denominator = jnp.concatenate(denom_parts, 0)
    numer_rows, denom_rows = (
        lax.psum_scatter(numerator, "head", scatter_dimension=1, tiled=True),
        lax.psum_scatter(denominator, "head", scatter_dimension=1, tiled=True),
    )
    token_attention = (numer_rows / denom_rows[..., None]).astype(jnp.bfloat16)
    clip_limit = clamp_code[0].astype(jnp.float32) / 1024.0
    scale_out = 1.0 / math.sqrt(head_count * head_dim)
    hd_matrix = hadamard(head_dim).astype(jnp.bfloat16)
    inner_mixed = jnp.einsum(
        "hrd,de->hre", token_attention, hd_matrix, preferred_element_type=jnp.float32
    )
    rotated = jnp.einsum(
        "gh,hre->gre", hadamard(head_count), inner_mixed, precision=lax.Precision.HIGHEST
    )
    clamped = jnp.clip(rotated * scale_out, -clip_limit, clip_limit).astype(jnp.bfloat16)
    activation = lax.all_to_all(clamped, "head", split_axis=0, concat_axis=1, tiled=True)[0]
    projected = lax.psum_scatter(
        lax.dot_general(
            w_out, activation, (((0,), (1,)), ((), ())), preferred_element_type=jnp.float32
        ),
        "head",
        scatter_dimension=0,
        tiled=True,
    )
    return projected.astype(jnp.bfloat16)


def solution(mesh):
    return jax.shard_map(
        per_device,
        mesh=mesh,
        in_specs=(
            P("groups", "head"),
            P(None, ("groups", "head"), None),
            P(None, None, ("groups", "head")),
            P("groups"),
            P("groups"),
            P("groups"),
            P("head", None),
        ),
        out_specs=P("head", "groups"),
        check_vma=False,
    )
```

profile of v0, /device:TPU:0, one launch (start us, length us, event | category | flops | bytes accessed | tf_op | source)
XLA Modules:
  0.0 251.2 jit_solution(6421445603097386101)
XLA Ops:
  6.5 0.0 copy-start
  6.5 0.0 reduce-scatter.4.cloned.1.call-start
  6.5 0.7 slice_convert_fusion
  7.3 0.7 convert_multiply_fusion
  7.9 0.9 copy.19
  8.8 24.6 %all_gather.3 = bf16[128,2048]{0,1:T(8,128)(2,1)S(1)} all-gather(bf16[128,128]{0,1:T(8,128)(2,1)S(1)} %copy.19), channel_id=1, replica_groups=mesh['groups'=2,'head'=16] {'head'}, dimensions={1}, use_global_device_ids=true | all-gather | bytes 557056 | tf_op jit(solution)/shard_map/all_gather | solution.py:38
  33.4 0.8 select_reduce_fusion
  34.2 0.1 compare_and_fusion
  34.3 1.3 fusion
  35.6 30.3 %pmax.7 = f32[16,128]{1,0:T(8,128)S(1)} all-reduce(f32[16,128]{1,0:T(8,128)S(1)} %get-tuple-element.7), channel_id=1, replica_groups=mesh['groups'=2,'head'=16] {'head'}, use_global_device_ids=true, to_apply=%region_3.4 | all-reduce | flops 2048 | bytes 16384 | tf_op jit(solution)/shard_map/pmax | solution.py:66
  65.9 0.0 copy-done
  65.9 0.0 copy-start.1
  66.0 1.9 fusion.5
  67.9 0.0 reduce-scatter.4.cloned.1.call-update
  67.9 0.0 reduce-scatter.6.cloned.1.call-start
  68.6 0.0 copy-done.1
  68.6 0.6 dynamic-slice
  69.9 0.6 fusion.1
  70.4 30.2 %all-reduce = f32[16,128]{1,0:T(8,128)S(1)} all-reduce(f32[16,128]{1,0:T(8,128)S(1)} %fusion.1), channel_id=3, replica_groups=mesh['groups'=2,'head'=16] {'head'}, use_global_device_ids=true, to_apply=%region_6.7.clone | all-reduce | flops 2048 | bytes 16384
  100.7 0.1 constant_dynamic-slice_fusion
  100.7 22.4 %reduce-scatter.4.cloned.1.call-done = f32[16,8,128]{2,1,0:T(8,128)} async-done(((f32[16,128,128]{2,1,0:T(8,128)}), f32[16,8,128]{2,1,0:T(8,128)}) %reduce-scatter.4.cloned.1.call-update) | async-done | bytes 65552 | tf_op jit(solution)/shard_map/reduce_scatter | solution.py:94
  123.1 0.9 divide_convert_fusion
  124.1 0.2 fusion.14
  124.3 0.2 fusion.4
  124.5 10.1 %all_to_all.4 = bf16[16,8,128]{2,1,0:T(8,128)(2,1)S(1)} all-to-all(bf16[16,8,128]{2,1,0:T(8,128)(2,1)S(1)} %copy.23), channel_id=1, replica_groups=mesh['groups'=2,'head'=16] {'head'}, dimensions={0} | all-to-all | bytes 65536 | tf_op jit(solution)/shard_map/all_to_all | solution.py:108
  134.6 6.7 %convolution_bitcast_fusion = f32[16384,128]{0,1:T(8,128)} fusion(bf16[128,16384]{1,0:T(8,128)(2,1)} %param.13, bf16[16,8,128]{2,1,0:T(8,128)(2,1)S(1)} %all_to_all.4), kind=kOutput, calls=%fused_computation | convolution fusion | flops 536870912 | bytes 12615680 | tf_op jit(solution)/shard_map/dot_general | solution.py:110
  141.3 0.0 reduce-scatter.6.cloned.1.call-update
  141.3 101.1 %reduce-scatter.6.cloned.1.call-done = f32[1024,128]{0,1:T(8,128)} async-done(((f32[16384,128]{0,1:T(8,128)}), f32[1024,128]{0,1:T(8,128)}) %reduce-scatter.6.cloned.1.call-update) | async-done | bytes 524304 | tf_op jit(solution)/shard_map/reduce_scatter | solution.py:109
  242.4 1.1 convert_element_type.32
  243.5 0.8 copy.24
  (4 shorter events, 0.0 us)
Async XLA Ops:
  6.5 59.4 %copy-start = (bf16[2,256,128]{2,1,0:T(8,128)(2,1)S(1)}, bf16[2,256,128]{2,1,0:T(8,128)(2,1)}, u32[]{:S(2)}) copy-start(bf16[2,256,128]{2,1,0:T(8,128)(2,1)} %param.8) | copy-start | bytes 393220
  6.5 116.6 %reduce-scatter.4.cloned.1.call-start = ((), (), s32[]{:S(2)}) async-start(), calls=%async_computation.3 | async-start | bytes 1114112 | tf_op jit(solution)/shard_map/reduce_scatter | solution.py:94
  65.9 2.7 %copy-start.1 = (u32[32]{0:T(128)S(1)}, u32[32]{0:T(128)}, u32[]{:S(2)}) copy-start(u32[32]{0:T(128)} %constant.97) | copy-start | bytes 388
  67.9 174.5 %reduce-scatter.6.cloned.1.call-start = ((), (), s32[]{:S(2)}) async-start(), calls=%async_computation.4 | async-start | bytes 8912896 | tf_op jit(solution)/shard_map/reduce_scatter | solution.py:109
Sparse Core Ops, SparseCore 0:
  68.0 55.0 reduce-scatter.3
  141.4 100.9 reduce-scatter.5
where the time goes:
time: 252 us; the launch traced here: 251 us
  waiting for transfers between devices  124 us (49%)
  blocking collectives  95.3 us (38%)
  between operations  14.8 us (6%)
  matrix products  10.3 us (4%)
  other arithmetic  4.83 us (2%)
    reduce_scatter x1, waiting for transfers between devices, per_device(): lax.psum_scatter(lax.dot_general(w_out, activation, (((0,), (1,)), ((), (...  101 us
    pmax x1, blocking collectives, per_device(): global_max = lax.pmax(local_max, 'head')  30.3 us
    unnamed x1, blocking collectives  30.2 us
    all_gather x1, blocking collectives, per_device(): gathered = lax.all_gather(queries, 'head', axis=1, tiled=True)  24.6 us
    reduce_scatter x1, waiting for transfers between devices, per_device(): lax.psum_scatter(numerator, 'head', scatter_dimension=1, tiled=True)  22.4 us
    all_to_all x1, blocking collectives, per_device(): lax.all_to_all(clamped, 'head', split_axis=0, concat_axis=1, tiled=True)[0]  10.1 us
    dot_general x1, matrix products, per_device(): lax.dot_general(w_out, activation, (((0,), (1,)), ((), ())), preferred_el...  6.66 us
  transfers between devices with their start and end apart: 2, of which 2 were waited for; matrix products, arithmetic and copies ran while one was open for 0% of the time, Pallas kernels for 0%

commit v1 on v0

--- a/solution.py
+++ b/solution.py
@@ -35,7 +35,12 @@
     head_dim = queries.shape[1]
     local_len = cache.shape[1]
     kv_count = cache.shape[2] // head_dim
-    gathered = lax.all_gather(queries, "head", axis=1, tiled=True)
+    ring = [queries]
+    for hop in range(15):
+        ring.append(lax.ppermute(ring[-1], "head", [(dev, (dev + 1) % 16) for dev in range(16)]))
+    gathered = jnp.roll(
+        jnp.concatenate(ring[::-1], axis=1), (lax.axis_index("head") + 1) * ring[0].shape[1], axis=1
+    )
     tok_rows = gathered.shape[0]
     head_count = gathered.shape[1] // head_dim
     per_group = head_count // kv_count

time: 252 us -> 316 us (1.25)
  waiting for transfers between devices: 124 us -> 212 us
  blocking collectives: 95.3 us -> 70.4 us
    ppermute x0 -> x15, waiting for transfers between devices: none -> 88.8 us  [per_device(): lax.ppermute(ring[-1], 'head', [(dev, (dev + 1) % 16) for dev in range(16)])]
    all_gather x1 -> x0, blocking collectives: 24.6 us -> none  [per_device(): gathered = lax.all_gather(queries, 'head', axis=1, tiled=True)]
  transfers between devices with their start and end apart: 2 -> 17, of which waited for: 2 -> 17; matrix products, arithmetic and copies ran while one was open for 0% -> 1% of each run, Pallas kernels for 0% -> 0%
where the time goes in v1:
time: 316 us
  waiting for transfers between devices  212 us (67%)
  blocking collectives  70.4 us (22%)
  between operations  15 us (5%)
  matrix products  9.38 us (3%)
  other arithmetic  5.08 us (2%)
    reduce_scatter x1, waiting for transfers between devices, per_device(): lax.psum_scatter(lax.dot_general(w_out, activation, (((0,), (1,)), ((), (...  101 us
    ppermute x15, waiting for transfers between devices, per_device(): lax.ppermute(ring[-1], 'head', [(dev, (dev + 1) % 16) for dev in range(16)])  88.8 us
    unnamed x1, blocking collectives  30.3 us
    pmax x1, blocking collectives, per_device(): global_max = lax.pmax(local_max, 'head')  30 us
    reduce_scatter x1, waiting for transfers between devices, per_device(): lax.psum_scatter(numerator, 'head', scatter_dimension=1, tiled=True)  22.5 us
    all_to_all x1, blocking collectives, per_device(): lax.all_to_all(clamped, 'head', split_axis=0, concat_axis=1, tiled=True)[0]  10.2 us
    dot_general x1, matrix products, per_device(): lax.dot_general(w_out, activation, (((0,), (1,)), ((), ())), preferred_el...  6.64 us
  transfers between devices with their start and end apart: 17, of which 17 were waited for; matrix products, arithmetic and copies ran while one was open for 1% of the time, Pallas kernels for 0%

profile of v1, /device:TPU:0, one launch (start us, length us, event | category | flops | bytes accessed | tf_op | source)
XLA Modules:
  0.0 315.7 jit_solution(4039181844055805137)
XLA Ops:
  6.5 0.0 copy-start
  6.5 0.0 reduce-scatter.4.cloned.1.call-start
  6.5 0.9 copy.22
  7.4 0.5 collective-permute-start
  8.0 6.6 %collective-permute-done = bf16[128,128]{0,1:T(8,128)(2,1)S(1)} collective-permute-done((bf16[128,128]{0,1:T(8,128)(2,1)S(1)}, bf16[128,128]{0,1:T(8,128)(2,1)S(1)}, u32[]{:S(2)}, u32[]{:S(2)}) %collective-permute-start) | collective-permute-done | bytes 32800 | tf_op jit(solution)/shard_map/ppermute | solution.py:40
  14.6 0.0 collective-permute-start.1
  14.6 6.0 %collective-permute-done.1 = bf16[128,128]{0,1:T(8,128)(2,1)S(1)} collective-permute-done((bf16[128,128]{0,1:T(8,128)(2,1)S(1)}, bf16[128,128]{0,1:T(8,128)(2,1)S(1)}, u32[]{:S(2)}, u32[]{:S(2)}) %collective-permute-start.1) | collective-permute-done | bytes 32800 | tf_op jit(solution)/shard_map/ppermute | solution.py:40
  20.6 0.0 collective-permute-start.2
  20.6 6.0 %collective-permute-done.2 = bf16[128,128]{0,1:T(8,128)(2,1)S(1)} collective-permute-done((bf16[128,128]{0,1:T(8,128)(2,1)S(1)}, bf16[128,128]{0,1:T(8,128)(2,1)S(1)}, u32[]{:S(2)}, u32[]{:S(2)}) %collective-permute-start.2) | collective-permute-done | bytes 32800 | tf_op jit(solution)/shard_map/ppermute | solution.py:40
  26.6 0.0 collective-permute-start.3
  26.6 6.0 %collective-permute-done.3 = bf16[128,128]{0,1:T(8,128)(2,1)S(1)} collective-permute-done((bf16[128,128]{0,1:T(8,128)(2,1)S(1)}, bf16[128,128]{0,1:T(8,128)(2,1)S(1)}, u32[]{:S(2)}, u32[]{:S(2)}) %collective-permute-start.3) | collective-permute-done | bytes 32800 | tf_op jit(solution)/shard_map/ppermute | solution.py:40
  32.7 0.0 collective-permute-start.4
  32.7 6.0 %collective-permute-done.4 = bf16[128,128]{0,1:T(8,128)(2,1)S(1)} collective-permute-done((bf16[128,128]{0,1:T(8,128)(2,1)S(1)}, bf16[128,128]{0,1:T(8,128)(2,1)S(1)}, u32[]{:S(2)}, u32[]{:S(2)}) %collective-permute-start.4) | collective-permute-done | bytes 32800 | tf_op jit(solution)/shard_map/ppermute | solution.py:40
  38.7 0.0 collective-permute-start.5
  38.7 6.0 %collective-permute-done.5 = bf16[128,128]{0,1:T(8,128)(2,1)S(1)} collective-permute-done((bf16[128,128]{0,1:T(8,128)(2,1)S(1)}, bf16[128,128]{0,1:T(8,128)(2,1)S(1)}, u32[]{:S(2)}, u32[]{:S(2)}) %collective-permute-start.5) | collective-permute-done | bytes 32800 | tf_op jit(solution)/shard_map/ppermute | solution.py:40
  44.8 0.0 collective-permute-start.6
  44.8 6.0 %collective-permute-done.6 = bf16[128,128]{0,1:T(8,128)(2,1)S(1)} collective-permute-done((bf16[128,128]{0,1:T(8,128)(2,1)S(1)}, bf16[128,128]{0,1:T(8,128)(2,1)S(1)}, u32[]{:S(2)}, u32[]{:S(2)}) %collective-permute-start.6) | collective-permute-done | bytes 32800 | tf_op jit(solution)/shard_map/ppermute | solution.py:40
  50.8 0.0 collective-permute-start.7
  50.8 6.0 %collective-permute-done.7 = bf16[128,128]{0,1:T(8,128)(2,1)S(1)} collective-permute-done((bf16[128,128]{0,1:T(8,128)(2,1)S(1)}, bf16[128,128]{0,1:T(8,128)(2,1)S(1)}, u32[]{:S(2)}, u32[]{:S(2)}) %collective-permute-start.7) | collective-permute-done | bytes 32800 | tf_op jit(solution)/shard_map/ppermute | solution.py:40
  56.8 0.0 collective-permute-start.8
  56.8 6.0 %collective-permute-done.8 = bf16[128,128]{0,1:T(8,128)(2,1)S(1)} collective-permute-done((bf16[128,128]{0,1:T(8,128)(2,1)S(1)}, bf16[128,128]{0,1:T(8,128)(2,1)S(1)}, u32[]{:S(2)}, u32[]{:S(2)}) %collective-permute-start.8) | collective-permute-done | bytes 32800 | tf_op jit(solution)/shard_map/ppermute | solution.py:40
  62.9 0.0 collective-permute-start.9
  62.9 0.8 select_reduce_fusion
  63.6 5.3 %collective-permute-done.9 = bf16[128,128]{0,1:T(8,128)(2,1)S(1)} collective-permute-done((bf16[128,128]{0,1:T(8,128)(2,1)S(1)}, bf16[128,128]{0,1:T(8,128)(2,1)S(1)}, u32[]{:S(2)}, u32[]{:S(2)}) %collective-permute-start.9) | collective-permute-done | bytes 32800 | tf_op jit(solution)/shard_map/ppermute | solution.py:40
  68.9 0.0 collective-permute-start.10
  68.9 6.0 %collective-permute-done.10 = bf16[128,128]{0,1:T(8,128)(2,1)S(1)} collective-permute-done((bf16[128,128]{0,1:T(8,128)(2,1)S(1)}, bf16[128,128]{0,1:T(8,128)(2,1)S(1)}, u32[]{:S(2)}, u32[]{:S(2)}) %collective-permute-start.10) | collective-permute-done | bytes 32800 | tf_op jit(solution)/shard_map/ppermute | solution.py:40
  74.9 0.0 collective-permute-start.11
  74.9 6.0 %collective-permute-done.11 = bf16[128,128]{0,1:T(8,128)(2,1)S(1)} collective-permute-done((bf16[128,128]{0,1:T(8,128)(2,1)S(1)}, bf16[128,128]{0,1:T(8,128)(2,1)S(1)}, u32[]{:S(2)}, u32[]{:S(2)}) %collective-permute-start.11) | collective-permute-done | bytes 32800 | tf_op jit(solution)/shard_map/ppermute | solution.py:40
  81.0 0.0 collective-permute-start.12
  81.0 0.1 compare_and_fusion
  81.1 5.9 %collective-permute-done.12 = bf16[128,128]{0,1:T(8,128)(2,1)S(1)} collective-permute-done((bf16[128,128]{0,1:T(8,128)(2,1)S(1)}, bf16[128,128]{0,1:T(8,128)(2,1)S(1)}, u32[]{:S(2)}, u32[]{:S(2)}) %collective-permute-start.12) | collective-permute-done | bytes 32800 | tf_op jit(solution)/shard_map/ppermute | solution.py:40
  87.0 0.0 collective-permute-start.13
  87.0 0.7 slice_convert_fusion
  87.7 5.3 %collective-permute-done.13 = bf16[128,128]{0,1:T(8,128)(2,1)S(1)} collective-permute-done((bf16[128,128]{0,1:T(8,128)(2,1)S(1)}, bf16[128,128]{0,1:T(8,128)(2,1)S(1)}, u32[]{:S(2)}, u32[]{:S(2)}) %collective-permute-start.13) | collective-permute-done | bytes 32800 | tf_op jit(solution)/shard_map/ppermute | solution.py:40
  93.1 0.0 collective-permute-start.14
  93.1 0.7 convert_multiply_fusion
  93.7 5.4 %collective-permute-done.14 = bf16[128,128]{0,1:T(8,128)(2,1)S(1)} collective-permute-done((bf16[128,128]{0,1:T(8,128)(2,1)S(1)}, bf16[128,128]{0,1:T(8,128)(2,1)S(1)}, u32[]{:S(2)}, u32[]{:S(2)}) %collective-permute-start.14) | collective-permute-done | bytes 32800 | tf_op jit(solution)/shard_map/ppermute | solution.py:40
  99.6 0.0 copy-done
  99.6 0.6 bitcast_reduce_fusion
  100.2 30.0 %pmax.7 = f32[16,128]{1,0:T(8,128)S(1)} all-reduce(f32[16,128]{1,0:T(8,128)S(1)} %get-tuple-element.7), channel_id=1, replica_groups=mesh['groups'=2,'head'=16] {'head'}, use_global_device_ids=true, to_apply=%region_3.4 | all-reduce | flops 2048 | bytes 16384 | tf_op jit(solution)/shard_map/pmax | solution.py:71
  130.2 0.0 copy-start.1
  130.2 1.7 fusion.6
  132.0 0.0 reduce-scatter.4.cloned.1.call-update
  132.0 0.0 reduce-scatter.6.cloned.1.call-start
  132.7 0.0 copy-done.1
  132.7 0.6 dynamic-slice
  133.9 0.8 fusion.2
  134.8 30.3 %all-reduce = f32[16,128]{1,0:T(8,128)S(1)} all-reduce(f32[16,128]{1,0:T(8,128)S(1)} %fusion.2), channel_id=3, replica_groups=mesh['groups'=2,'head'=16] {'head'}, use_global_device_ids=true, to_apply=%region_6.7.clone | all-reduce | flops 2048 | bytes 16384
  165.0 0.1 constant_dynamic-slice_fusion
  165.1 22.5 %reduce-scatter.4.cloned.1.call-done = f32[16,8,128]{2,1,0:T(8,128)} async-done(((f32[16,128,128]{2,1,0:T(8,128)}), f32[16,8,128]{2,1,0:T(8,128)}) %reduce-scatter.4.cloned.1.call-update) | async-done | bytes 65552 | tf_op jit(solution)/shard_map/reduce_scatter | solution.py:99
  187.6 0.9 divide_convert_fusion
  188.5 0.2 fusion.17
  188.7 0.2 fusion.5
  189.0 10.2 %all_to_all.4 = bf16[16,8,128]{2,1,0:T(8,128)(2,1)S(1)} all-to-all(bf16[16,8,128]{2,1,0:T(8,128)(2,1)S(1)} %copy.27), channel_id=1, replica_groups=mesh['groups'=2,'head'=16] {'head'}, dimensions={0} | all-to-all | bytes 65536 | tf_op jit(solution)/shard_map/all_to_all | solution.py:113
  199.1 6.6 %convolution_bitcast_fusion = f32[16384,128]{0,1:T(8,128)} fusion(bf16[128,16384]{1,0:T(8,128)(2,1)} %param.13, bf16[16,8,128]{2,1,0:T(8,128)(2,1)S(1)} %all_to_all.4), kind=kOutput, calls=%fused_computation | convolution fusion | flops 536870912 | bytes 12615680 | tf_op jit(solution)/shard_map/dot_general | solution.py:115
  205.8 0.0 reduce-scatter.6.cloned.1.call-update
  205.8 101.1 %reduce-scatter.6.cloned.1.call-done = f32[1024,128]{0,1:T(8,128)} async-done(((f32[16384,128]{0,1:T(8,128)}), f32[1024,128]{0,1:T(8,128)}) %reduce-scatter.6.cloned.1.call-update) | async-done | bytes 524304 | tf_op jit(solution)/shard_map/reduce_scatter | solution.py:114
  306.9 1.1 convert_element_type.32
  308.0 0.8 copy.28
  (37 shorter events, 0.4 us)
Async XLA Ops:
  6.5 93.1 %copy-start = (bf16[2,256,128]{2,1,0:T(8,128)(2,1)S(1)}, bf16[2,256,128]{2,1,0:T(8,128)(2,1)}, u32[]{:S(2)}) copy-start(bf16[2,256,128]{2,1,0:T(8,128)(2,1)} %param.8) | copy-start | bytes 393220
  6.5 181.1 %reduce-scatter.4.cloned.1.call-start = ((), (), s32[]{:S(2)}) async-start(), calls=%async_computation.3 | async-start | bytes 1114112 | tf_op jit(solution)/shard_map/reduce_scatter | solution.py:99
  7.4 7.1 %collective-permute-start = (bf16[128,128]{0,1:T(8,128)(2,1)S(1)}, bf16[128,128]{0,1:T(8,128)(2,1)S(1)}, u32[]{:S(2)}, u32[]{:S(2)}) collective-permute-start(bf16[128,128]{0,1:T(8,128)(2,1)S(1)} %copy.22), channel_id=1, source_target_pairs={{0,1},{1,2},{2,3},{3,4},{4,5},{5,6},{6,7},{7,8},{8,9},{9,10},{10,1... | collective-permute-start | bytes 98312 | tf_op jit(solution)/shard_map/ppermute | solution.py:40
  14.6 6.0 %collective-permute-start.1 = (bf16[128,128]{0,1:T(8,128)(2,1)S(1)}, bf16[128,128]{0,1:T(8,128)(2,1)S(1)}, u32[]{:S(2)}, u32[]{:S(2)}) collective-permute-start(bf16[128,128]{0,1:T(8,128)(2,1)S(1)} %collective-permute-done), channel_id=1, source_target_pairs={{0,1},{1,2},{2,3},{3,4},{4,5},{5,6},{6,7},{7,8},{8,9},{9,10},{10,1... | collective-permute-start | bytes 98312 | tf_op jit(solution)/shard_map/ppermute | solution.py:40
  20.6 6.0 %collective-permute-start.2 = (bf16[128,128]{0,1:T(8,128)(2,1)S(1)}, bf16[128,128]{0,1:T(8,128)(2,1)S(1)}, u32[]{:S(2)}, u32[]{:S(2)}) collective-permute-start(bf16[128,128]{0,1:T(8,128)(2,1)S(1)} %collective-permute-done.1), channel_id=1, source_target_pairs={{0,1},{1,2},{2,3},{3,4},{4,5},{5,6},{6,7},{7,8},{8,9},{9,10},{10,1... | collective-permute-start | bytes 98312 | tf_op jit(solution)/shard_map/ppermute | solution.py:40
  26.6 6.0 %collective-permute-start.3 = (bf16[128,128]{0,1:T(8,128)(2,1)S(1)}, bf16[128,128]{0,1:T(8,128)(2,1)S(1)}, u32[]{:S(2)}, u32[]{:S(2)}) collective-permute-start(bf16[128,128]{0,1:T(8,128)(2,1)S(1)} %collective-permute-done.2), channel_id=1, source_target_pairs={{0,1},{1,2},{2,3},{3,4},{4,5},{5,6},{6,7},{7,8},{8,9},{9,10},{10,1... | collective-permute-start | bytes 98312 | tf_op jit(solution)/shard_map/ppermute | solution.py:40
  32.7 6.0 %collective-permute-start.4 = (bf16[128,128]{0,1:T(8,128)(2,1)S(1)}, bf16[128,128]{0,1:T(8,128)(2,1)S(1)}, u32[]{:S(2)}, u32[]{:S(2)}) collective-permute-start(bf16[128,128]{0,1:T(8,128)(2,1)S(1)} %collective-permute-done.3), channel_id=1, source_target_pairs={{0,1},{1,2},{2,3},{3,4},{4,5},{5,6},{6,7},{7,8},{8,9},{9,10},{10,1... | collective-permute-start | bytes 98312 | tf_op jit(solution)/shard_map/ppermute | solution.py:40
  38.7 6.0 %collective-permute-start.5 = (bf16[128,128]{0,1:T(8,128)(2,1)S(1)}, bf16[128,128]{0,1:T(8,128)(2,1)S(1)}, u32[]{:S(2)}, u32[]{:S(2)}) collective-permute-start(bf16[128,128]{0,1:T(8,128)(2,1)S(1)} %collective-permute-done.4), channel_id=1, source_target_pairs={{0,1},{1,2},{2,3},{3,4},{4,5},{5,6},{6,7},{7,8},{8,9},{9,10},{10,1... | collective-permute-start | bytes 98312 | tf_op jit(solution)/shard_map/ppermute | solution.py:40
  44.8 6.0 %collective-permute-start.6 = (bf16[128,128]{0,1:T(8,128)(2,1)S(1)}, bf16[128,128]{0,1:T(8,128)(2,1)S(1)}, u32[]{:S(2)}, u32[]{:S(2)}) collective-permute-start(bf16[128,128]{0,1:T(8,128)(2,1)S(1)} %collective-permute-done.5), channel_id=1, source_target_pairs={{0,1},{1,2},{2,3},{3,4},{4,5},{5,6},{6,7},{7,8},{8,9},{9,10},{10,1... | collective-permute-start | bytes 98312 | tf_op jit(solution)/shard_map/ppermute | solution.py:40
  50.8 6.0 %collective-permute-start.7 = (bf16[128,128]{0,1:T(8,128)(2,1)S(1)}, bf16[128,128]{0,1:T(8,128)(2,1)S(1)}, u32[]{:S(2)}, u32[]{:S(2)}) collective-permute-start(bf16[128,128]{0,1:T(8,128)(2,1)S(1)} %collective-permute-done.6), channel_id=1, source_target_pairs={{0,1},{1,2},{2,3},{3,4},{4,5},{5,6},{6,7},{7,8},{8,9},{9,10},{10,1... | collective-permute-start | bytes 98312 | tf_op jit(solution)/shard_map/ppermute | solution.py:40
  56.8 6.0 %collective-permute-start.8 = (bf16[128,128]{0,1:T(8,128)(2,1)S(1)}, bf16[128,128]{0,1:T(8,128)(2,1)S(1)}, u32[]{:S(2)}, u32[]{:S(2)}) collective-permute-start(bf16[128,128]{0,1:T(8,128)(2,1)S(1)} %collective-permute-done.7), channel_id=1, source_target_pairs={{0,1},{1,2},{2,3},{3,4},{4,5},{5,6},{6,7},{7,8},{8,9},{9,10},{10,1... | collective-permute-start | bytes 98312 | tf_op jit(solution)/shard_map/ppermute | solution.py:40
  62.9 6.0 %collective-permute-start.9 = (bf16[128,128]{0,1:T(8,128)(2,1)S(1)}, bf16[128,128]{0,1:T(8,128)(2,1)S(1)}, u32[]{:S(2)}, u32[]{:S(2)}) collective-permute-start(bf16[128,128]{0,1:T(8,128)(2,1)S(1)} %collective-permute-done.8), channel_id=1, source_target_pairs={{0,1},{1,2},{2,3},{3,4},{4,5},{5,6},{6,7},{7,8},{8,9},{9,10},{10,1... | collective-permute-start | bytes 98312 | tf_op jit(solution)/shard_map/ppermute | solution.py:40
  68.9 6.0 %collective-permute-start.10 = (bf16[128,128]{0,1:T(8,128)(2,1)S(1)}, bf16[128,128]{0,1:T(8,128)(2,1)S(1)}, u32[]{:S(2)}, u32[]{:S(2)}) collective-permute-start(bf16[128,128]{0,1:T(8,128)(2,1)S(1)} %collective-permute-done.9), channel_id=1, source_target_pairs={{0,1},{1,2},{2,3},{3,4},{4,5},{5,6},{6,7},{7,8},{8,9},{9,10},{10,1... | collective-permute-start | bytes 98312 | tf_op jit(solution)/shard_map/ppermute | solution.py:40
  74.9 6.0 %collective-permute-start.11 = (bf16[128,128]{0,1:T(8,128)(2,1)S(1)}, bf16[128,128]{0,1:T(8,128)(2,1)S(1)}, u32[]{:S(2)}, u32[]{:S(2)}) collective-permute-start(bf16[128,128]{0,1:T(8,128)(2,1)S(1)} %collective-permute-done.10), channel_id=1, source_target_pairs={{0,1},{1,2},{2,3},{3,4},{4,5},{5,6},{6,7},{7,8},{8,9},{9,10},{10,1... | collective-permute-start | bytes 98312 | tf_op jit(solution)/shard_map/ppermute | solution.py:40
  81.0 6.0 %collective-permute-start.12 = (bf16[128,128]{0,1:T(8,128)(2,1)S(1)}, bf16[128,128]{0,1:T(8,128)(2,1)S(1)}, u32[]{:S(2)}, u32[]{:S(2)}) collective-permute-start(bf16[128,128]{0,1:T(8,128)(2,1)S(1)} %collective-permute-done.11), channel_id=1, source_target_pairs={{0,1},{1,2},{2,3},{3,4},{4,5},{5,6},{6,7},{7,8},{8,9},{9,10},{10,1... | collective-permute-start | bytes 98312 | tf_op jit(solution)/shard_map/ppermute | solution.py:40
  87.0 6.0 %collective-permute-start.13 = (bf16[128,128]{0,1:T(8,128)(2,1)S(1)}, bf16[128,128]{0,1:T(8,128)(2,1)S(1)}, u32[]{:S(2)}, u32[]{:S(2)}) collective-permute-start(bf16[128,128]{0,1:T(8,128)(2,1)S(1)} %collective-permute-done.12), channel_id=1, source_target_pairs={{0,1},{1,2},{2,3},{3,4},{4,5},{5,6},{6,7},{7,8},{8,9},{9,10},{10,1... | collective-permute-start | bytes 98312 | tf_op jit(solution)/shard_map/ppermute | solution.py:40
  93.1 6.0 %collective-permute-start.14 = (bf16[128,128]{0,1:T(8,128)(2,1)S(1)}, bf16[128,128]{0,1:T(8,128)(2,1)S(1)}, u32[]{:S(2)}, u32[]{:S(2)}) collective-permute-start(bf16[128,128]{0,1:T(8,128)(2,1)S(1)} %collective-permute-done.13), channel_id=1, source_target_pairs={{0,1},{1,2},{2,3},{3,4},{4,5},{5,6},{6,7},{7,8},{8,9},{9,10},{10,1... | collective-permute-start | bytes 98312 | tf_op jit(solution)/shard_map/ppermute | solution.py:40
  130.2 2.5 copy-start.1
  132.0 174.9 %reduce-scatter.6.cloned.1.call-start = ((), (), s32[]{:S(2)}) async-start(), calls=%async_computation.4 | async-start | bytes 8912896 | tf_op jit(solution)/shard_map/reduce_scatter | solution.py:114
Sparse Core Ops, SparseCore 0:
  132.1 55.4 reduce-scatter.3
  205.9 100.9 reduce-scatter.5
